TPU v7x, 32 devices: a whole 2x2x4 slice. The times are simulated.
32 devices in a mesh: grp: 4 (over x, core), var: 8 (over z, y).
Axes of the slice: x: 2, y: 2, z: 4, core: 2. Of those that a mesh axis runs over, the one named last changes fastest.
Arguments:
- dosages: int32 [16384, 8192], P('grp', 'var'), may hold values from 0 to 2
- variant_weight: bfloat16 [8192], P('var'), may hold values from -2 to 2
- block_id: int32 [8192], P('var'), may hold values from 0 to 127
- stack_weight: bfloat16 [1024, 64], replicated, may hold values from -0.1875 to 0.1875
- labels: int32 [16384, 64], P(('grp', 'var')), may hold values 0 or 1
Outputs:
- level_grad: float32 [1024, 64], P('var')
- weight_grad: float32 [8192], P('var')
All inputs are finite; a program needn't handle non-finite values. No bound on the sum of `labels` on one device may be relied on, other than what follows from the above.
Results may differ from a plain program's by a relative error of at most 0.00039.
Values may be sent and summed in bfloat16 or wider, within the bound.
A program may use at most 64 MiB of HBM per device.

v0:
```python
import math
import jax
import jax.numpy as jnp
from jax import lax
from jax.sharding import PartitionSpec as P


def owned_level(predictors, group_resid, norm_scale):
    owned = (
        lax.dot_general(
            predictors, group_resid, (((0,), (0,)), ((), ())), preferred_element_type=jnp.float32
        )
        * norm_scale
    )
    return lax.psum(owned, "grp")


def local(dosages, variant_weight, block_id, stack_weight, labels):
    person_rows = dosages.shape[0]
    total_preds = stack_weight.shape[0]
    var_count = lax.axis_size("var")
    per_device = total_preds // var_count
    norm_scale = 1.0 / math.sqrt(person_rows * lax.axis_size("grp"))
    dose_vals = dosages.astype(jnp.bfloat16)
    one_hot = block_id[:, None] == lax.iota(jnp.int32, per_device)[None, :]
    weighted = jnp.where(one_hot, variant_weight[:, None], jnp.zeros((), jnp.bfloat16))
    predictors = jnp.dot(dose_vals, weighted, preferred_element_type=jnp.float32).astype(
        jnp.bfloat16
    )
    regrouped = None
    regrouped = lax.all_to_all(predictors, "var", split_axis=0, concat_axis=1, tiled=True)
    logits = jnp.dot(regrouped, stack_weight, preferred_element_type=jnp.float32)
    resid = (jax.nn.sigmoid(logits) - labels.astype(jnp.float32)).astype(jnp.bfloat16)
    group_resid = None
    group_resid = lax.all_gather(resid, "var", axis=0, tiled=True)
    level_grad = owned_level(predictors, group_resid, norm_scale)
    full_grad = lax.dot_general(
        resid, stack_weight, (((1,), (1,)), ((), ())), preferred_element_type=jnp.float32
    ).astype(jnp.bfloat16)
    local_grad = lax.all_to_all(full_grad, "var", split_axis=1, concat_axis=0, tiled=True)
    column_grad = lax.dot_general(
        dose_vals, local_grad, (((0,), (0,)), ((), ())), preferred_element_type=jnp.float32
    )
    local_weight = jnp.sum(jnp.where(one_hot, column_grad, 0.0), axis=1) * norm_scale
    weight_grad = lax.psum(local_weight, "grp")
    return (level_grad, weight_grad)


def solution(mesh):
    return jax.shard_map(
        local,
        mesh=mesh,
        in_specs=(P("grp", "var"), P("var"), P("var"), P(), P(("grp", "var"), None)),
        out_specs=(P("var", None), P("var")),
        check_vma=False,
    )
```

profile of v0, /device:TPU:0, one launch (start us, length us, event | category | flops | bytes accessed | tf_op | source)
XLA Modules:
  0.0 113.5 jit_solution(6263934042086971203)
XLA Ops:
  0.6 0.0 copy-start
  0.6 0.0 copy-start.2
  0.7 8.8 %convolution_convert_fusion = bf16[128,4096]{1,0:T(8,128)(2,1)S(1)} fusion(s32[4096,1024]{1,0:T(8,128)} %param.5, s32[1024]{0:T(1024)} %param.7, bf16[1024]{0:T(1024)(128)(2,1)} %param.6), kind=kOutput, calls=%fused_computation | convolution fusion | flops 1078722560 | bytes 17831936 | tf_op jit(solution)/shard_map/dot_general | solution.py:27
  9.4 0.0 copy-start.1
  9.4 0.1 copy.14
  9.5 32.9 %all_to_all.38 = bf16[8,512,128]{1,2,0:T(8,128)(2,1)S(1)} all-to-all(bf16[8,512,128]{1,2,0:T(8,128)(2,1)S(1)} %bitcast.31), channel_id=1, replica_groups=mesh['grp'=4,'var'=8] {'var'}, dimensions={0} | all-to-all | bytes 2097152 | tf_op jit(solution)/shard_map/all_to_all | solution.py:31
  42.4 0.0 copy-done
  42.4 0.0 copy-done.2
  42.4 0.3 fusion.17
  42.8 0.4 fusion.3
  43.2 1.2 %copy.13 = bf16[64,8,8,128]{3,2,0,1:T(8,128)(2,1)} copy(bf16[64,8,8,128]{3,2,1,0:T(8,128)(2,1)S(1)} %fusion.3) | data formatting | bytes 2097152 | tf_op jit(solution)/shard_map/all_to_all | solution.py:40
  44.4 3.6 %all-to-all-start.1 = ((bf16[512,8,128]{2,0,1:T(8,128)(2,1)}), bf16[512,8,128]{2,0,1:T(8,128)(2,1)S(1)}, u32[]{:S(2)}, u32[]{:S(2)}) async-start(bf16[512,8,128]{2,0,1:T(8,128)(2,1)} %bitcast.27), calls=%async_computation.1 | async-start | bytes 2097152 | tf_op jit(solution)/shard_map/all_to_all | solution.py:40
  48.0 46.9 %all_gather.3 = bf16[4096,64]{0,1:T(8,128)(2,1)S(1)} all-gather(bf16[512,64]{0,1:T(8,128)(2,1)S(1)} %fusion.17), channel_id=1, replica_groups=mesh['grp'=4,'var'=8] {'var'}, dimensions={0}, use_global_device_ids=true | all-gather | bytes 589824 | tf_op jit(solution)/shard_map/all_gather | solution.py:35
  94.9 0.5 convolution_multiply_fusion
  95.4 0.0 all-to-all-done.1
  95.4 0.0 copy-done.1
  95.4 7.1 %fusion.10 = f32[1024]{0:T(1024)S(1)} fusion(bf16[4096,128]{1,0:T(8,128)(2,1)S(1)} %bitcast.30, s32[4096,1024]{1,0:T(8,128)} %param.5, s32[1024]{0:T(1024)S(1)} %copy-done.1), kind=kOutput, calls=%fused_computation.8 | convolution fusion | flops 1078328320 | bytes 17833984 | tf_op jit(solution)/shard_map/dot_general | solution.py:41
  102.5 11.1 %all-reduce = (f32[128,64]{0,1:T(8,128)}, f32[1024]{0:T(1024)}) all-reduce(f32[128,64]{0,1:T(8,128)S(1)} %convolution_multiply_fusion, f32[1024]{0:T(1024)S(1)} %broadcast_multiply_fusion), channel_id=1, replica_groups=mesh['grp'=4,'var'=8] {'grp'}, use_global_device_ids=true, to_apply=%region_0.1 | all-reduce | flops 9216 | bytes 73728 | tf_op jit(solution)/shard_map/psum | solution.py:15
  (1 shorter events, 0.0 us)
Async XLA Ops:
  0.6 41.8 %copy-start = (bf16[1024,64]{0,1:T(8,128)(2,1)S(1)}, bf16[1024,64]{0,1:T(8,128)(2,1)}, u32[]{:S(2)}) copy-start(bf16[1024,64]{0,1:T(8,128)(2,1)} %param.8) | copy-start | bytes 393220
  0.6 41.8 %copy-start.2 = (s32[512,64]{0,1:T(8,128)S(1)}, s32[512,64]{0,1:T(8,128)}, u32[]{:S(2)}) copy-start(s32[512,64]{0,1:T(8,128)} %param.9) | copy-start | bytes 393220
  9.4 86.0 %copy-start.1 = (s32[1024]{0:T(1024)S(1)}, s32[1024]{0:T(1024)}, u32[]{:S(2)}) copy-start(s32[1024]{0:T(1024)} %param.7) | copy-start | bytes 12292
  44.4 51.0 %all-to-all-start.1 = ((bf16[512,8,128]{2,0,1:T(8,128)(2,1)}), bf16[512,8,128]{2,0,1:T(8,128)(2,1)S(1)}, u32[]{:S(2)}, u32[]{:S(2)}) async-start(bf16[512,8,128]{2,0,1:T(8,128)(2,1)} %bitcast.27), calls=%async_computation.1 | async-start | bytes 2097152 | tf_op jit(solution)/shard_map/all_to_all | solution.py:40
where the time goes:
time: 114 us
  blocking collectives  90.8 us (80%)
  matrix products  17.1 us (15%)
  starting transfers between devices  3.6 us (3%)
  local copies, waits for them, and re-layouts  1.29 us (1%)
    all_gather x1, blocking collectives, local(): group_resid = lax.all_gather(resid, 'var', axis=0, tiled=True)  46.9 us
    all_to_all x1, blocking collectives, local(): lax.all_to_all(predictors, 'var', split_axis=0, concat_axis=1, tiled=True)  32.9 us
    psum x1, blocking collectives, owned_level(): return lax.psum(owned, 'grp')  11.1 us
    dot_general x1, matrix products, local(): jnp.dot(dose_vals, weighted, preferred_element_type=jnp.float32)  8.76 us
    dot_general x1, matrix products, local(): lax.dot_general(dose_vals, local_grad, (((0,), (0,)), ((), ())), preferre...  7.06 us
    all_to_all x1, starting transfers between devices, local(): lax.all_to_all(full_grad, 'var', split_axis=1, concat_axis=0, tiled=True)  3.6 us
  transfers between devices with their start and end apart: 1, of which 0 were waited for; matrix products, arithmetic and copies ran while one was open for 0% of the time, Pallas kernels for 0%

commit v1 on v0

--- a/solution.py
+++ b/solution.py
@@ -28,7 +28,10 @@
         jnp.bfloat16
     )
     regrouped = None
-    regrouped = lax.all_to_all(predictors, "var", split_axis=0, concat_axis=1, tiled=True)
+    regrouped = jnp.concatenate(
+        lax.all_to_all(jnp.stack(jnp.split(predictors, lax.axis_size("var"), axis=0)), "var", 0, 0),
+        axis=1,
+    )
     logits = jnp.dot(regrouped, stack_weight, preferred_element_type=jnp.float32)
     resid = (jax.nn.sigmoid(logits) - labels.astype(jnp.float32)).astype(jnp.bfloat16)
     group_resid = None

time: 114 us -> 114 us (level)
  no operation moved by 1% of the time
where the time goes in v1:
time: 114 us
  blocking collectives  90.8 us (80%)
  matrix products  17.1 us (15%)
  starting transfers between devices  3.6 us (3%)
  local copies, waits for them, and re-layouts  1.29 us (1%)
    all_gather x1, blocking collectives, local(): group_resid = lax.all_gather(resid, 'var', axis=0, tiled=True)  46.9 us
    all_to_all x1, blocking collectives, local(): lax.all_to_all(jnp.stack(jnp.split(predictors, lax.axis_size('var'), axis...  32.9 us
    psum x1, blocking collectives, owned_level(): return lax.psum(owned, 'grp')  11.1 us
    dot_general x1, matrix products, local(): jnp.dot(dose_vals, weighted, preferred_element_type=jnp.float32)  8.76 us
    dot_general x1, matrix products, local(): lax.dot_general(dose_vals, local_grad, (((0,), (0,)), ((), ())), preferre...  7.06 us
    all_to_all x1, starting transfers between devices, local(): lax.all_to_all(full_grad, 'var', split_axis=1, concat_axis=0, tiled=True)  3.6 us
  transfers between devices with their start and end apart: 1, of which 0 were waited for; matrix products, arithmetic and copies ran while one was open for 0% of the time, Pallas kernels for 0%

profile of v1, /device:TPU:0, one launch (start us, length us, event | category | flops | bytes accessed | tf_op | source)
XLA Modules:
  0.0 113.6 jit_solution(9358059204479928694)
XLA Ops:
  0.6 0.0 copy-start
  0.6 0.0 copy-start.2
  0.7 8.8 %convolution_convert_fusion = bf16[128,4096]{1,0:T(8,128)(2,1)S(1)} fusion(s32[4096,1024]{1,0:T(8,128)} %param.5, s32[1024]{0:T(1024)} %param.7, bf16[1024]{0:T(1024)(128)(2,1)} %param.6), kind=kOutput, calls=%fused_computation | convolution fusion | flops 1078722560 | bytes 17831936 | tf_op jit(solution)/shard_map/dot_general | solution.py:27
  9.4 0.0 copy-start.1
  9.6 32.9 %all_to_all.24 = bf16[8,512,128]{1,2,0:T(8,128)(2,1)S(1)} all-to-all(bf16[8,512,128]{1,2,0:T(8,128)(2,1)S(1)} %fusion.21), channel_id=1, replica_groups=mesh['grp'=4,'var'=8] {'var'}, dimensions={0} | all-to-all | bytes 2097152 | tf_op jit(solution)/shard_map/all_to_all | solution.py:32
  42.5 0.0 copy-done
  42.5 0.0 copy-done.2
  42.5 0.3 fusion.17
  42.8 0.4 fusion.3
  43.3 1.2 %copy.10 = bf16[64,8,8,128]{3,2,0,1:T(8,128)(2,1)} copy(bf16[64,8,8,128]{3,2,1,0:T(8,128)(2,1)S(1)} %fusion.3) | data formatting | bytes 2097152 | tf_op jit(solution)/shard_map/all_to_all | solution.py:43
  44.4 3.6 %all-to-all-start.1 = ((bf16[512,8,128]{2,0,1:T(8,128)(2,1)}), bf16[512,8,128]{2,0,1:T(8,128)(2,1)S(1)}, u32[]{:S(2)}, u32[]{:S(2)}) async-start(bf16[512,8,128]{2,0,1:T(8,128)(2,1)} %bitcast.56), calls=%async_computation.1 | async-start | bytes 2097152 | tf_op jit(solution)/shard_map/all_to_all | solution.py:43
  48.0 46.9 %all_gather.3 = bf16[4096,64]{0,1:T(8,128)(2,1)S(1)} all-gather(bf16[512,64]{0,1:T(8,128)(2,1)S(1)} %fusion.17), channel_id=1, replica_groups=mesh['grp'=4,'var'=8] {'var'}, dimensions={0}, use_global_device_ids=true | all-gather | bytes 589824 | tf_op jit(solution)/shard_map/all_gather | solution.py:38
  94.9 0.5 convolution_multiply_fusion
  95.4 0.0 all-to-all-done.1
  95.4 0.0 copy-done.1
  95.4 7.1 %fusion.10 = f32[1024]{0:T(1024)S(1)} fusion(bf16[4096,128]{1,0:T(8,128)(2,1)S(1)} %bitcast.65, s32[4096,1024]{1,0:T(8,128)} %param.5, s32[1024]{0:T(1024)S(1)} %copy-done.1), kind=kOutput, calls=%fused_computation.8 | convolution fusion | flops 1078328320 | bytes 17833984 | tf_op jit(solution)/shard_map/dot_general | solution.py:44
  102.5 11.1 %all-reduce = (f32[128,64]{0,1:T(8,128)}, f32[1024]{0:T(1024)}) all-reduce(f32[128,64]{0,1:T(8,128)S(1)} %convolution_multiply_fusion, f32[1024]{0:T(1024)S(1)} %broadcast_multiply_fusion), channel_id=1, replica_groups=mesh['grp'=4,'var'=8] {'grp'}, use_global_device_ids=true, to_apply=%region_0.1 | all-reduce | flops 9216 | bytes 73728 | tf_op jit(solution)/shard_map/psum | solution.py:15
  (9 shorter events, 0.1 us)
Async XLA Ops:
  0.6 41.8 %copy-start = (bf16[1024,64]{0,1:T(8,128)(2,1)S(1)}, bf16[1024,64]{0,1:T(8,128)(2,1)}, u32[]{:S(2)}) copy-start(bf16[1024,64]{0,1:T(8,128)(2,1)} %param.8) | copy-start | bytes 393220
  0.6 41.8 %copy-start.2 = (s32[512,64]{0,1:T(8,128)S(1)}, s32[512,64]{0,1:T(8,128)}, u32[]{:S(2)}) copy-start(s32[512,64]{0,1:T(8,128)} %param.9) | copy-start | bytes 393220
  9.4 86.0 %copy-start.1 = (s32[1024]{0:T(1024)S(1)}, s32[1024]{0:T(1024)}, u32[]{:S(2)}) copy-start(s32[1024]{0:T(1024)} %param.7) | copy-start | bytes 12292
  44.4 51.0 %all-to-all-start.1 = ((bf16[512,8,128]{2,0,1:T(8,128)(2,1)}), bf16[512,8,128]{2,0,1:T(8,128)(2,1)S(1)}, u32[]{:S(2)}, u32[]{:S(2)}) async-start(bf16[512,8,128]{2,0,1:T(8,128)(2,1)} %bitcast.56), calls=%async_computation.1 | async-start | bytes 2097152 | tf_op jit(solution)/shard_map/all_to_all | solution.py:43
